TPU v7x, 32 devices: a whole 2x2x4 slice. The times are simulated.
32 devices in a mesh: rows: 8 (over z, y), modes: 4 (over x, core).
Axes of the slice: x: 2, y: 2, z: 4, core: 2. Of those that a mesh axis runs over, the one named last changes fastest.
Arguments:
- mode_slab: bfloat16 [4096, 512], P('rows', 'modes'), may hold values from -25 to 25
- mass_diag: float32 [4096], P('rows'), may hold values from 9.5 to 19
- mass_gain: float32 [4096], P('rows'), may hold values from 0.5 to 1.5
- band_coef: float32 [4], replicated, may hold values from 0.2 to 0.5
- band_offsets: int32 [4], replicated, may hold values from 1 to 64, as said below
- boundary_blocks: int32 [16, 4], P('rows'), may hold values from 0 to 31, as said below
- boundary_counts: int32 [16], P('rows'), may hold values from 2 to 4, as said below
- boundary_modes: bfloat16 [16, 512, 512], P('rows'), may hold values from -0.5 to 0.5
Outputs:
- projected: bfloat16 [16, 512, 512], P('rows', 'modes')
Inputs may be any that keep to these rules, and one draw needn't show every extreme that they name: `band_offsets`: the offsets are distinct and one of them equals 64. `boundary_blocks`: entries of one component are distinct. For component c with e = c // 2, every entry b (used or not) satisfies (b - e * 4 + 512 // 256) mod (32) < 8. Among the used entries of the components of each index e of rows, one is the block just below e's rows and one the block just above them, counted cyclically. `boundary_counts`: some component uses all 4 blocks.
All inputs are finite; a program needn't handle non-finite values.
Results may differ from a plain program's by a relative error of at most 0.0035.
The roundings to bfloat16 on the way count: a program that leaves them out, or rounds other values in their place, can miss the bound.
Values may be sent and summed in bfloat16 or wider, within the bound.
No kernel may reach another device: no remote copies, remote signals or barrier semaphores. Data moves between devices by JAX's collectives and lax.ppermute only.
A program may use at most 64 MiB of HBM per device.

v0:
```python
import jax
import jax.numpy as jnp
from jax import lax
from jax.sharding import PartitionSpec as P

CB = 512
BLOCK = 128
BMAX = 4
NOFF = 4
BAND = 64


def padded_2(block, sides, width, periodic):
    for axis, dim in sides:
        count = lax.axis_size(axis)
        forward = [(i, i + 1) for i in range(count - 1)]
        if periodic:
            forward.append((count - 1, 0))
        backward = [(target, source) for source, target in forward]
        low = lax.ppermute(
            lax.slice_in_dim(block, block.shape[dim] - width, None, axis=dim), axis, forward
        )
        high = lax.ppermute(lax.slice_in_dim(block, 0, width, axis=dim), axis, backward)
        block = jnp.concatenate([low, block, high], axis=dim)
    return block


def local(
    mode_slab,
    mass_diag,
    mass_gain,
    band_coef,
    band_offsets,
    boundary_blocks,
    boundary_counts,
    boundary_modes,
):
    rows_dev, mode_cols = mode_slab.shape
    per_dev = rows_dev // BLOCK
    rim_rows = per_dev // 2 * BLOCK
    slab_float = mode_slab.astype(jnp.float32)
    scaled = (mass_gain[:, None] * slab_float).astype(jnp.bfloat16)
    padded = padded_2(scaled, (("rows", 0),), BAND, False)
    neighbour = jnp.zeros((rows_dev, mode_cols), jnp.float32)
    for j in range(NOFF):
        offset = band_offsets[j]
        upward = lax.dynamic_slice_in_dim(padded, BAND + offset, rows_dev, 0)
        downward = lax.dynamic_slice_in_dim(padded, BAND - offset, rows_dev, 0)
        neighbour = neighbour + band_coef[j] * (
            upward.astype(jnp.float32) + downward.astype(jnp.float32)
        )
    mass_image = (mass_diag[:, None] * slab_float + mass_gain[:, None] * neighbour).astype(
        jnp.bfloat16
    )
    every_mode = lax.all_gather(mass_image, "modes", axis=1, tiled=True)
    full_order = every_mode.shape[1]
    total_rows = rows_dev * lax.axis_size("rows")
    partial_value = (
        lax.dot_general(
            every_mode, mode_slab, (((0,), (0,)), ((), ())), preferred_element_type=jnp.float32
        )
        / total_rows
    )
    column_block = lax.psum(partial_value, "rows")
    gram_matrix = lax.all_gather(column_block, "modes", axis=1, tiled=True)
    lower_factor = jnp.linalg.cholesky(gram_matrix)
    first_column = lax.axis_index("modes") * mode_cols
    unit_columns = (
        lax.broadcasted_iota(jnp.int32, (full_order, mode_cols), 0)
        == lax.broadcasted_iota(jnp.int32, (full_order, mode_cols), 1) + first_column
    ).astype(jnp.float32)
    inverse = jax.scipy.linalg.solve_triangular(
        lower_factor, unit_columns, lower=True, trans=1
    ).astype(jnp.bfloat16)
    mass_basis = jnp.dot(every_mode, inverse, preferred_element_type=jnp.float32).astype(
        jnp.bfloat16
    )
    extended = padded_2(mass_basis, (("rows", 0),), rim_rows, True)
    total_blocks = per_dev * lax.axis_size("rows")
    window_start = lax.axis_index("rows") * per_dev - per_dev // 2
    local_blocks = jnp.mod(boundary_blocks - window_start, total_blocks)
    owned = boundary_modes.shape[0]
    shaped = boundary_modes.reshape(owned, BMAX, BLOCK, CB)
    row_index = local_blocks[:, :, None] * BLOCK + jnp.arange(BLOCK, dtype=jnp.int32)[None, None, :]
    picked = jnp.take(extended, row_index, axis=0)
    in_use = jnp.arange(BMAX, dtype=jnp.int32)[None, :] < boundary_counts[:, None]
    picked = jnp.where(in_use[:, :, None, None], picked, jnp.zeros_like(picked))
    result = jnp.einsum("csbk,csbm->ckm", picked, shaped, preferred_element_type=jnp.float32)
    return result.astype(jnp.bfloat16)


def solution(mesh):
    in_specs = (
        P("rows", "modes"),
        P("rows"),
        P("rows"),
        P(),
        P(),
        P("rows", None),
        P("rows"),
        P("rows", None, None),
    )
    out_specs = P("rows", "modes", None)
    return jax.shard_map(local, mesh=mesh, in_specs=in_specs, out_specs=out_specs, check_vma=False)
```

profile of v0, /device:TPU:0, one launch (start us, length us, event | category | flops | bytes accessed | tf_op | source)
XLA Modules:
  0.0 294.4 jit_solution(5894387732189599143)
XLA Ops:
  7.7 4.9 %collective-permute-start = (bf16[64,128]{1,0:T(8,128)(2,1)S(1)}, bf16[64,128]{1,0:T(8,128)(2,1)S(1)}, u32[]{:S(2)}, u32[]{:S(2)}) collective-permute-start(bf16[64,128]{1,0:T(8,128)(2,1)S(1)} %get-tuple-element.25), channel_id=1, source_target_pairs={{0,4},{4,8},{8,12},{12,16},{16,20},{20,24},{24,28},{1,5},{5,9},{9,... | collective-permute-start | bytes 49160 | tf_op jit(solution)/shard_map/ppermute | solution.py:20
  26.4 2.8 fusion.3
  29.2 7.2 %all_gather.6 = bf16[512,512]{1,0:T(8,128)(2,1)S(1)} all-gather(bf16[512,128]{1,0:T(8,128)(2,1)S(1)} %fusion.3), channel_id=1, replica_groups=mesh['rows'=8,'modes'=4] {'modes'}, dimensions={1}, use_global_device_ids=true | all-gather | bytes 655360 | tf_op jit(solution)/shard_map/all_gather | solution.py:55
  38.3 72.4 %all-reduce.3.cloned.1.call-done = f32[512,128]{0,1:T(8,128)} async-done(((f32[512,128]{0,1:T(8,128)}), f32[512,128]{0,1:T(8,128)}) %all-reduce.3.cloned.1.call-update) | async-done | bytes 262160 | tf_op jit(solution)/shard_map/psum | solution.py:64
  112.8 15.5 %all-gather.2.cloned.1.call-done = f32[512,512]{0,1:T(8,128)} async-done(((f32[512,128]{0,1:T(8,128)}), f32[512,512]{0,1:T(8,128)}) %all-gather.2.cloned.1.call-update) | async-done | bytes 1048592 | tf_op jit(solution)/shard_map/all_gather | solution.py:65
  128.4 1.6 copy.13
  131.3 11.7 %cholesky.104 = f32[128,128]{1,0:T(8,128)S(1)} custom-call(f32[128,128]{1,0:T(8,128)S(1)} %cholesky.266), custom_call_target="Cholesky" | custom-call | tf_op jit(solution)/shard_map/jit(cholesky)/cholesky | solution.py:66
  143.1 9.8 %custom-call.31 = f32[1,128,128]{1,2,0:T(8,128)S(1)} custom-call(f32[1,128,128]{2,1,0:T(8,128)S(1)} %get-tuple-element.36), custom_call_target="InvertDiagBlocksLowerTriangular" | custom-call | tf_op jit(solution)/shard_map/jit(cholesky)/cholesky | solution.py:66
  154.3 11.7 %cholesky.217 = f32[128,128]{1,0:T(8,128)S(1)} custom-call(f32[128,128]{1,0:T(8,128)S(1)} %cholesky.270), custom_call_target="Cholesky" | custom-call | tf_op jit(solution)/shard_map/jit(cholesky)/cholesky | solution.py:66
  166.1 9.9 %custom-call.32 = f32[1,128,128]{1,2,0:T(8,128)S(1)} custom-call(f32[1,128,128]{2,1,0:T(8,128)S(1)} %get-tuple-element.33), custom_call_target="InvertDiagBlocksLowerTriangular" | custom-call | tf_op jit(solution)/shard_map/jit(cholesky)/cholesky | solution.py:66
  178.2 13.2 %cholesky.238 = f32[128,128]{1,0:T(8,128)} custom-call(f32[128,128]{1,0:T(8,128)} %cholesky.275), custom_call_target="Cholesky" | custom-call | tf_op jit(solution)/shard_map/jit(cholesky)/cholesky | solution.py:66
  191.4 1.5 select_reduce_fusion.1
  193.6 11.3 %custom-call.33 = f32[1,128,128]{1,2,0:T(8,128)} custom-call(f32[1,128,128]{2,1,0:T(8,128)} %get-tuple-element.30), custom_call_target="InvertDiagBlocksLowerTriangular" | custom-call | tf_op jit(solution)/shard_map/jit(cholesky)/cholesky | solution.py:66
  206.3 11.7 %cholesky.255 = f32[128,128]{1,0:T(8,128)S(1)} custom-call(f32[128,128]{1,0:T(8,128)S(1)} %convolution_subtract_fusion.5), custom_call_target="Cholesky" | custom-call | tf_op jit(solution)/shard_map/jit(cholesky)/cholesky | solution.py:66
  222.8 9.9 %while.1 = (s32[]{:T(128)}, f32[512,512]{1,0:T(8,128)S(1)}, s32[4,2]{0,1:T(2,128)S(1)}, f32[4,128,128]{2,1,0:T(8,128)}, s32[]{:T(128)}) while((s32[]{:T(128)}, f32[512,512]{1,0:T(8,128)S(1)}, s32[4,2]{0,1:T(2,128)S(1)}, f32[4,128,128]{2,1,0:T(8,128)}, s32[]{:T(128)}) %tuple.39), condition=%wide.while_cond, body=%wide.while_body.sunk | while | flops 2 | bytes 132705 | solution.py:72
  223.4 1.9 bitcast_dynamic-update-slice_fusion.2
  225.8 1.9 bitcast_dynamic-update-slice_fusion.2
  228.3 1.9 bitcast_dynamic-update-slice_fusion.2
  230.8 1.9 bitcast_dynamic-update-slice_fusion.2
  232.6 40.1 %custom-call.34 = f32[4,128,128]{1,2,0:T(8,128)S(1)} custom-call(f32[4,128,128]{2,1,0:T(8,128)} %get-tuple-element.12), custom_call_target="InvertDiagBlocksLowerTriangular" | custom-call | tf_op jit(solution)/shard_map/jit(_solve_triangular)/triangular_solve | solution.py:72
  275.9 1.5 collective-permute-start.2
  277.4 3.3 %collective-permute-start.3 = (bf16[256,128]{1,0:T(8,128)(2,1)S(1)}, bf16[256,128]{1,0:T(8,128)(2,1)S(1)}, u32[]{:S(2)}, u32[]{:S(2)}) collective-permute-start(bf16[256,128]{1,0:T(8,128)(2,1)S(1)} %get-tuple-element.24), channel_id=1, source_target_pairs={{4,0},{8,4},{12,8},{16,12},{20,16},{24,20},{28,24},{0,28},{5,1},{9... | collective-permute-start | bytes 196616 | tf_op jit(solution)/shard_map/ppermute | solution.py:23
  280.8 2.2 collective-permute-done.2
  283.1 3.2 %gather_fusion = bf16[1024,128]{1,0:T(8,128)(2,1)S(1)} fusion(bf16[1024,128]{1,0:T(8,128)(2,1)S(1)} %pad_maximum_fusion, s32[1024]{0:T(1024)S(1)} %broadcast_clamp_fusion), kind=kCustom, calls=%fused_computation | custom fusion | bytes 528384 | tf_op jit(solution)/shard_map/jit(_take)/gather | solution.py:85
  (92 shorter events, 24.8 us)
Async XLA Ops:
  6.5 280.0 %copy-start = (bf16[2,512,512]{2,1,0:T(8,128)(2,1)S(1)}, bf16[2,512,512]{2,1,0:T(8,128)(2,1)}, u32[]{:S(2)}) copy-start(bf16[2,512,512]{2,1,0:T(8,128)(2,1)} %param.15) | copy-start | bytes 3145732
  6.5 104.1 %all-reduce.3.cloned.1.call-start = ((), (), s32[]{:S(2)}) async-start(), calls=%async_computation | async-start | bytes 524288 | tf_op jit(solution)/shard_map/psum | solution.py:64
  7.7 6.2 %copy-start.9 = (s32[4]{0:T(128)S(1)}, s32[4]{0:T(128)}, u32[]{:S(2)}) copy-start(s32[4]{0:T(128)} %param.12) | copy-start | bytes 52
  7.7 17.8 %collective-permute-start = (bf16[64,128]{1,0:T(8,128)(2,1)S(1)}, bf16[64,128]{1,0:T(8,128)(2,1)S(1)}, u32[]{:S(2)}, u32[]{:S(2)}) collective-permute-start(bf16[64,128]{1,0:T(8,128)(2,1)S(1)} %get-tuple-element.25), channel_id=1, source_target_pairs={{0,4},{4,8},{8,12},{12,16},{16,20},{20,24},{24,28},{1,5},{5,9},{9,... | collective-permute-start | bytes 49160 | tf_op jit(solution)/shard_map/ppermute | solution.py:20
  12.6 12.9 %collective-permute-start.1 = (bf16[64,128]{1,0:T(8,128)(2,1)S(1)}, bf16[64,128]{1,0:T(8,128)(2,1)S(1)}, u32[]{:S(2)}, u32[]{:S(2)}) collective-permute-start(bf16[64,128]{1,0:T(8,128)(2,1)S(1)} %get-tuple-element.26), channel_id=1, source_target_pairs={{4,0},{8,4},{12,8},{16,12},{20,16},{24,20},{28,24},{5,1},{9,5},{13... | collective-permute-start | bytes 49160 | tf_op jit(solution)/shard_map/ppermute | solution.py:23
  13.9 0.7 copy-start.10
  25.5 0.9 copy-start.6
  25.6 0.9 copy-start.11
  25.6 0.8 copy-start.8
  36.4 0.8 copy-start.4
  38.3 90.1 %all-gather.2.cloned.1.call-start = ((), (), s32[]{:S(2)}) async-start(), calls=%async_computation.1 | async-start | bytes 1310720 | tf_op jit(solution)/shard_map/all_gather | solution.py:65
  111.3 0.7 copy-start.12
  128.4 1.7 copy-start.1
  130.2 1.0 copy-start.2
  131.2 21.7 %copy-start.3 = (f32[512,512]{1,0:T(8,128)S(1)}, f32[512,512]{1,0:T(8,128)}, u32[]{:S(2)}) copy-start(f32[512,512]{1,0:T(8,128)} %copy-done.2) | copy-start | bytes 3145732
  153.6 0.7 copy-start.7
  222.1 0.7 copy-start.14
  274.5 1.0 copy-start.5
  275.9 4.8 %copy-start.13 = (s32[2]{0:T(128)S(1)}, s32[2]{0:T(128)}, u32[]{:S(2)}) copy-start(s32[2]{0:T(128)} %param.14) | copy-start | bytes 28
  275.9 7.1 %collective-permute-start.2 = (bf16[256,128]{1,0:T(8,128)(2,1)S(1)}, bf16[256,128]{1,0:T(8,128)(2,1)S(1)}, u32[]{:S(2)}, u32[]{:S(2)}) collective-permute-start(bf16[256,128]{1,0:T(8,128)(2,1)S(1)} %get-tuple-element.23), channel_id=1, source_target_pairs={{0,4},{4,8},{8,12},{12,16},{16,20},{20,24},{24,28},{28,0},{1,5},{5... | collective-permute-start | bytes 196616 | tf_op jit(solution)/shard_map/ppermute | solution.py:20
  277.4 5.7 %collective-permute-start.3 = (bf16[256,128]{1,0:T(8,128)(2,1)S(1)}, bf16[256,128]{1,0:T(8,128)(2,1)S(1)}, u32[]{:S(2)}, u32[]{:S(2)}) collective-permute-start(bf16[256,128]{1,0:T(8,128)(2,1)S(1)} %get-tuple-element.24), channel_id=1, source_target_pairs={{4,0},{8,4},{12,8},{16,12},{20,16},{24,20},{28,24},{0,28},{5,1},{9... | collective-permute-start | bytes 196616 | tf_op jit(solution)/shard_map/ppermute | solution.py:23
Sparse Core Ops, SparseCore 0:
  38.4 72.2 all-reduce.2
  112.3 15.9 all-gather.1
where the time goes:
time: 295 us; the launch traced here: 294 us
  other arithmetic  129 us (44%)
  waiting for transfers between devices  90.3 us (31%)
  between operations  26.6 us (9%)
  local copies, waits for them, and re-layouts  21.7 us (7%)
  starting transfers between devices  11 us (4%)
  matrix products  8.59 us (3%)
  blocking collectives  7.2 us (2%)
    another operation x14, other arithmetic, local(): lower_factor = jnp.linalg.cholesky(gram_matrix)  83.2 us
    psum x1, waiting for transfers between devices, local(): column_block = lax.psum(partial_value, 'rows')  72.4 us
    another operation x3, other arithmetic, local(): jax.scipy.linalg.solve_triangular(lower_factor, unit_columns, lower=True,...  40.8 us
    all_gather x1, waiting for transfers between devices, local(): gram_matrix = lax.all_gather(column_block, 'modes', axis=1, tiled=True)  15.5 us
    another operation x12, local copies, waits for them, and re-layouts  9.85 us
    all_gather x1, blocking collectives, local(): every_mode = lax.all_gather(mass_image, 'modes', axis=1, tiled=True)  7.2 us
    ppermute x2, starting transfers between devices, padded_2(): lax.ppermute(lax.slice_in_dim(block, block.shape[dim] - width, None, axis...  6.39 us
  transfers between devices with their start and end apart: 6, of which 4 were waited for; matrix products, arithmetic and copies ran while one was open for 1% of the time, Pallas kernels for 0%

commit v1 on v0

--- a/solution.py
+++ b/solution.py
@@ -62,7 +62,14 @@
         / total_rows
     )
     column_block = lax.psum(partial_value, "rows")
-    gram_matrix = lax.all_gather(column_block, "modes", axis=1, tiled=True)
+    ring = [column_block]
+    for hop in range(3):
+        ring.append(lax.ppermute(ring[-1], "modes", [(dev, (dev + 1) % 4) for dev in range(4)]))
+    gram_matrix = jnp.roll(
+        jnp.concatenate(ring[::-1], axis=1),
+        (lax.axis_index("modes") + 1) * ring[0].shape[1],
+        axis=1,
+    )
     lower_factor = jnp.linalg.cholesky(gram_matrix)
     first_column = lax.axis_index("modes") * mode_cols
     unit_columns = (

time: 295 us -> 294 us (level)
  other arithmetic: 129 us -> 126 us
    ppermute x0 -> x3, waiting for transfers between devices: none -> 17.4 us  [local(): lax.ppermute(ring[-1], 'modes', [(dev, (dev + 1) % 4) for dev in range(4)])]
    all_gather x1 -> x0, waiting for transfers between devices: 15.5 us -> none  [local(): gram_matrix = lax.all_gather(column_block, 'modes', axis=1, tiled=True)]
    another operation x14, other arithmetic: 83.2 us -> 78.7 us  [local(): lower_factor = jnp.linalg.cholesky(gram_matrix)]
  transfers between devices with their start and end apart: 6 -> 8, of which waited for: 4 -> 5; matrix products, arithmetic and copies ran while one was open for 1% -> 1% of each run, Pallas kernels for 0% -> 0%
where the time goes in v1:
time: 294 us; the launch traced here: 293 us
  other arithmetic  126 us (43%)
  waiting for transfers between devices  92 us (31%)
  between operations  26.4 us (9%)
  local copies, waits for them, and re-layouts  20.9 us (7%)
  starting transfers between devices  10.9 us (4%)
  matrix products  9.77 us (3%)
  blocking collectives  7.2 us (2%)
    another operation x14, other arithmetic, local(): lower_factor = jnp.linalg.cholesky(gram_matrix)  78.7 us
    psum x1, waiting for transfers between devices, local(): column_block = lax.psum(partial_value, 'rows')  72.4 us
    another operation x3, other arithmetic, local(): jax.scipy.linalg.solve_triangular(lower_factor, unit_columns, lower=True,...  40.2 us
    ppermute x3, waiting for transfers between devices, local(): lax.ppermute(ring[-1], 'modes', [(dev, (dev + 1) % 4) for dev in range(4)])  17.4 us
    another operation x12, local copies, waits for them, and re-layouts  10.8 us
    all_gather x1, blocking collectives, local(): every_mode = lax.all_gather(mass_image, 'modes', axis=1, tiled=True)  7.2 us
  transfers between devices with their start and end apart: 8, of which 5 were waited for; matrix products, arithmetic and copies ran while one was open for 1% of the time, Pallas kernels for 0%

profile of v1, /device:TPU:0, one launch (start us, length us, event | category | flops | bytes accessed | tf_op | source)
XLA Modules:
  0.0 292.8 jit_solution(7338169038316625728)
XLA Ops:
  7.7 4.9 %collective-permute-start = (bf16[64,128]{1,0:T(8,128)(2,1)S(1)}, bf16[64,128]{1,0:T(8,128)(2,1)S(1)}, u32[]{:S(2)}, u32[]{:S(2)}) collective-permute-start(bf16[64,128]{1,0:T(8,128)(2,1)S(1)} %get-tuple-element.25), channel_id=1, source_target_pairs={{0,4},{4,8},{8,12},{12,16},{16,20},{20,24},{24,28},{1,5},{5,9},{9,... | collective-permute-start | bytes 49160 | tf_op jit(solution)/shard_map/ppermute | solution.py:20
  15.3 1.5 fusion.58
  27.0 3.9 %fusion.3 = bf16[512,128]{1,0:T(8,128)(2,1)S(1)} fusion(bf16[512,128]{1,0:T(8,128)(2,1)} %param.8, bf16[640,128]{1,0:T(8,128)(2,1)S(1)} %pad_maximum_fusion.1, s32[]{:T(128)S(6)} %select_n.80, s32[]{:T(128)S(6)} %select_n.79, f32[]{:T(128)} %bitcast.15, s32[]{:T(128)S(6)} %select_n.78, s32[]{:T(128)S(6)} %select_n.77, f32[]{:T(128)} %bitcast.10, ...), kind=kLoop, calls=%fused_computation.23 | loop fusion | flops 1572864 | bytes 1314864 | tf_op jit(solution)/shard_map/convert_element_type | solution.py:52
  30.8 7.2 %all_gather.3 = bf16[512,512]{1,0:T(8,128)(2,1)S(1)} all-gather(bf16[512,128]{1,0:T(8,128)(2,1)S(1)} %fusion.3), channel_id=1, replica_groups=mesh['rows'=8,'modes'=4] {'modes'}, dimensions={1}, use_global_device_ids=true | all-gather | bytes 655360 | tf_op jit(solution)/shard_map/all_gather | solution.py:55
  39.9 72.4 %all-reduce.3.cloned.1.call-done = f32[512,128]{0,1:T(8,128)} async-done(((f32[512,128]{0,1:T(8,128)}), f32[512,128]{0,1:T(8,128)}) %all-reduce.3.cloned.1.call-update) | async-done | bytes 262160 | tf_op jit(solution)/shard_map/psum | solution.py:64
  112.4 5.9 %collective-permute-done.2 = f32[512,128]{0,1:T(8,128)S(1)} collective-permute-done((f32[512,128]{0,1:T(8,128)}, f32[512,128]{0,1:T(8,128)S(1)}, u32[]{:S(2)}, u32[]{:S(2)}) %collective-permute-start.2) | collective-permute-done | bytes 262176 | tf_op jit(solution)/shard_map/ppermute | solution.py:67
  118.3 5.8 %collective-permute-done.3 = f32[512,128]{0,1:T(8,128)S(1)} collective-permute-done((f32[512,128]{0,1:T(8,128)S(1)}, f32[512,128]{0,1:T(8,128)S(1)}, u32[]{:S(2)}, u32[]{:S(2)}) %collective-permute-start.3) | collective-permute-done | bytes 262176 | tf_op jit(solution)/shard_map/ppermute | solution.py:67
  124.2 5.7 %collective-permute-done.4 = f32[512,128]{0,1:T(8,128)S(1)} collective-permute-done((f32[512,128]{0,1:T(8,128)S(1)}, f32[512,128]{0,1:T(8,128)S(1)}, u32[]{:S(2)}, u32[]{:S(2)}) %collective-permute-start.4) | collective-permute-done | bytes 262176 | tf_op jit(solution)/shard_map/ppermute | solution.py:67
  134.2 11.7 %cholesky.104 = f32[128,128]{1,0:T(8,128)S(1)} custom-call(f32[128,128]{1,0:T(8,128)S(1)} %cholesky.266), custom_call_target="Cholesky" | custom-call | tf_op jit(solution)/shard_map/jit(cholesky)/cholesky | solution.py:73
  146.1 9.8 %custom-call.31 = f32[1,128,128]{1,2,0:T(8,128)S(1)} custom-call(f32[1,128,128]{2,1,0:T(8,128)S(1)} %get-tuple-element.36), custom_call_target="InvertDiagBlocksLowerTriangular" | custom-call | tf_op jit(solution)/shard_map/jit(cholesky)/cholesky | solution.py:73
  158.5 11.7 %cholesky.217 = f32[128,128]{1,0:T(8,128)S(1)} custom-call(f32[128,128]{1,0:T(8,128)S(1)} %cholesky.270), custom_call_target="Cholesky" | custom-call | tf_op jit(solution)/shard_map/jit(cholesky)/cholesky | solution.py:73
  170.2 9.9 %custom-call.32 = f32[1,128,128]{1,2,0:T(8,128)S(1)} custom-call(f32[1,128,128]{2,1,0:T(8,128)S(1)} %get-tuple-element.33), custom_call_target="InvertDiagBlocksLowerTriangular" | custom-call | tf_op jit(solution)/shard_map/jit(cholesky)/cholesky | solution.py:73
  181.7 11.7 %cholesky.238 = f32[128,128]{1,0:T(8,128)S(1)} custom-call(f32[128,128]{1,0:T(8,128)S(1)} %cholesky.275), custom_call_target="Cholesky" | custom-call | tf_op jit(solution)/shard_map/jit(cholesky)/cholesky | solution.py:73
  194.1 9.8 %custom-call.33 = f32[1,128,128]{1,2,0:T(8,128)S(1)} custom-call(f32[1,128,128]{2,1,0:T(8,128)S(1)} %get-tuple-element.30), custom_call_target="InvertDiagBlocksLowerTriangular" | custom-call | tf_op jit(solution)/shard_map/jit(cholesky)/cholesky | solution.py:73
  205.4 11.9 %cholesky.255 = f32[128,128]{1,0:T(8,128)S(1)} custom-call(f32[128,128]{1,0:T(8,128)S(1)} %convolution_subtract_fusion.5), custom_call_target="Cholesky" | custom-call | tf_op jit(solution)/shard_map/jit(cholesky)/cholesky | solution.py:73
  221.2 10.8 %while.1 = (s32[]{:T(128)}, f32[512,512]{1,0:T(8,128)S(1)}, s32[4,2]{0,1:T(2,128)S(1)}, f32[4,128,128]{2,1,0:T(8,128)}, s32[]{:T(128)}) while((s32[]{:T(128)}, f32[512,512]{1,0:T(8,128)S(1)}, s32[4,2]{0,1:T(2,128)S(1)}, f32[4,128,128]{2,1,0:T(8,128)}, s32[]{:T(128)}) %tuple.39), condition=%wide.while_cond, body=%wide.while_body.sunk | while | flops 2 | bytes 132705 | solution.py:79
  221.9 2.0 bitcast_dynamic-update-slice_fusion.2
  224.6 2.0 bitcast_dynamic-update-slice_fusion.2
  227.3 2.0 bitcast_dynamic-update-slice_fusion.2
  230.0 2.0 bitcast_dynamic-update-slice_fusion.2
  232.0 40.1 %custom-call.34 = f32[4,128,128]{1,2,0:T(8,128)S(1)} custom-call(f32[4,128,128]{2,1,0:T(8,128)} %get-tuple-element.12), custom_call_target="InvertDiagBlocksLowerTriangular" | custom-call | tf_op jit(solution)/shard_map/jit(_solve_triangular)/triangular_solve | solution.py:79
  275.3 4.0 %collective-permute-start.6 = (bf16[256,128]{1,0:T(8,128)(2,1)S(1)}, bf16[256,128]{1,0:T(8,128)(2,1)S(1)}, u32[]{:S(2)}, u32[]{:S(2)}) collective-permute-start(bf16[256,128]{1,0:T(8,128)(2,1)S(1)} %get-tuple-element.24), channel_id=1, source_target_pairs={{4,0},{8,4},{12,8},{16,12},{20,16},{24,20},{28,24},{0,28},{5,1},{9... | collective-permute-start | bytes 196616 | tf_op jit(solution)/shard_map/ppermute | solution.py:23
  279.3 2.2 collective-permute-done.5
  281.5 3.2 %gather_fusion = bf16[1024,128]{1,0:T(8,128)(2,1)S(1)} fusion(bf16[1024,128]{1,0:T(8,128)(2,1)S(1)} %pad_maximum_fusion, s32[1024]{0:T(1024)S(1)} %broadcast_clamp_fusion), kind=kCustom, calls=%fused_computation | custom fusion | bytes 528384 | tf_op jit(solution)/shard_map/jit(_take)/gather | solution.py:92
  (92 shorter events, 25.1 us)
Async XLA Ops:
  6.5 278.4 %copy-start = (bf16[2,512,512]{2,1,0:T(8,128)(2,1)S(1)}, bf16[2,512,512]{2,1,0:T(8,128)(2,1)}, u32[]{:S(2)}) copy-start(bf16[2,512,512]{2,1,0:T(8,128)(2,1)} %param.15) | copy-start | bytes 3145732
  6.5 32.3 %copy-start.5 = (bf16[512,128]{1,0:T(8,128)(2,1)S(1)}, bf16[512,128]{1,0:T(8,128)(2,1)}, u32[]{:S(2)}) copy-start(bf16[512,128]{1,0:T(8,128)(2,1)} %param.8) | copy-start | bytes 393220
  6.5 33.3 %copy-start.7 = (s32[2,4]{1,0:T(2,128)S(1)}, s32[2,4]{1,0:T(2,128)}, u32[]{:S(2)}) copy-start(s32[2,4]{1,0:T(2,128)} %param.13) | copy-start | bytes 100
  6.5 105.7 %all-reduce.3.cloned.1.call-start = ((), (), s32[]{:S(2)}) async-start(), calls=%async_computation | async-start | bytes 524288 | tf_op jit(solution)/shard_map/psum | solution.py:64
  7.7 19.2 %collective-permute-start = (bf16[64,128]{1,0:T(8,128)(2,1)S(1)}, bf16[64,128]{1,0:T(8,128)(2,1)S(1)}, u32[]{:S(2)}, u32[]{:S(2)}) collective-permute-start(bf16[64,128]{1,0:T(8,128)(2,1)S(1)} %get-tuple-element.25), channel_id=1, source_target_pairs={{0,4},{4,8},{8,12},{12,16},{16,20},{20,24},{24,28},{1,5},{5,9},{9,... | collective-permute-start | bytes 49160 | tf_op jit(solution)/shard_map/ppermute | solution.py:20
  12.6 14.4 %collective-permute-start.1 = (bf16[64,128]{1,0:T(8,128)(2,1)S(1)}, bf16[64,128]{1,0:T(8,128)(2,1)S(1)}, u32[]{:S(2)}, u32[]{:S(2)}) collective-permute-start(bf16[64,128]{1,0:T(8,128)(2,1)S(1)} %get-tuple-element.26), channel_id=1, source_target_pairs={{4,0},{8,4},{12,8},{16,12},{20,16},{24,20},{28,24},{5,1},{9,5},{13... | collective-permute-start | bytes 49160 | tf_op jit(solution)/shard_map/ppermute | solution.py:23
  38.0 0.8 copy-start.3
  112.3 17.7 %copy-start.6 = (f32[512,128]{0,1:T(8,128)S(1)}, f32[512,128]{0,1:T(8,128)}, u32[]{:S(2)}) copy-start(f32[512,128]{0,1:T(8,128)} %all-reduce.3.cloned.1.call-done) | copy-start | bytes 786436
  112.3 6.0 %collective-permute-start.2 = (f32[512,128]{0,1:T(8,128)}, f32[512,128]{0,1:T(8,128)S(1)}, u32[]{:S(2)}, u32[]{:S(2)}) collective-permute-start(f32[512,128]{0,1:T(8,128)} %all-reduce.3.cloned.1.call-done), channel_id=1, source_target_pairs={{0,1},{1,2},{2,3},{3,0},{4,5},{5,6},{6,7},{7,4},{8,9},{9,10},{10,1... | collective-permute-start | bytes 786440 | tf_op jit(solution)/shard_map/ppermute | solution.py:67
  118.3 5.8 %collective-permute-start.3 = (f32[512,128]{0,1:T(8,128)S(1)}, f32[512,128]{0,1:T(8,128)S(1)}, u32[]{:S(2)}, u32[]{:S(2)}) collective-permute-start(f32[512,128]{0,1:T(8,128)S(1)} %collective-permute-done.2), channel_id=1, source_target_pairs={{0,1},{1,2},{2,3},{3,0},{4,5},{5,6},{6,7},{7,4},{8,9},{9,10},{10,1... | collective-permute-start | bytes 786440 | tf_op jit(solution)/shard_map/ppermute | solution.py:67
  124.1 5.8 %collective-permute-start.4 = (f32[512,128]{0,1:T(8,128)S(1)}, f32[512,128]{0,1:T(8,128)S(1)}, u32[]{:S(2)}, u32[]{:S(2)}) collective-permute-start(f32[512,128]{0,1:T(8,128)S(1)} %collective-permute-done.3), channel_id=1, source_target_pairs={{0,1},{1,2},{2,3},{3,0},{4,5},{5,6},{6,7},{7,4},{8,9},{9,10},{10,1... | collective-permute-start | bytes 786440 | tf_op jit(solution)/shard_map/ppermute | solution.py:67
  130.1 1.3 copy-start.2
  133.3 1.0 copy-start.1
  221.2 53.0 %copy-start.4 = (bf16[512,512]{1,0:T(8,128)(2,1)S(1)}, bf16[512,512]{1,0:T(8,128)(2,1)}, u32[]{:S(2)}) copy-start(bf16[512,512]{1,0:T(8,128)(2,1)} %copy-done.3) | copy-start | bytes 1572868
  221.2 58.1 %copy-start.8 = (s32[2]{0:T(128)S(1)}, s32[2]{0:T(128)}, u32[]{:S(2)}) copy-start(s32[2]{0:T(128)} %param.14) | copy-start | bytes 28
  274.5 7.0 %collective-permute-start.5 = (bf16[256,128]{1,0:T(8,128)(2,1)S(1)}, bf16[256,128]{1,0:T(8,128)(2,1)S(1)}, u32[]{:S(2)}, u32[]{:S(2)}) collective-permute-start(bf16[256,128]{1,0:T(8,128)(2,1)S(1)} %get-tuple-element.23), channel_id=1, source_target_pairs={{0,4},{4,8},{8,12},{12,16},{16,20},{20,24},{24,28},{28,0},{1,5},{5... | collective-permute-start | bytes 196616 | tf_op jit(solution)/shard_map/ppermute | solution.py:20
  275.3 6.2 %collective-permute-start.6 = (bf16[256,128]{1,0:T(8,128)(2,1)S(1)}, bf16[256,128]{1,0:T(8,128)(2,1)S(1)}, u32[]{:S(2)}, u32[]{:S(2)}) collective-permute-start(bf16[256,128]{1,0:T(8,128)(2,1)S(1)} %get-tuple-element.24), channel_id=1, source_target_pairs={{4,0},{8,4},{12,8},{16,12},{20,16},{24,20},{28,24},{0,28},{5,1},{9... | collective-permute-start | bytes 196616 | tf_op jit(solution)/shard_map/ppermute | solution.py:23
Sparse Core Ops, SparseCore 0:
  40.0 72.2 all-reduce.2
